TPU v7x, 256 devices: a whole 4x4x8 slice. The times are simulated.
256 devices in a mesh: pipe: 16 (over y_hi, z), vocab: 16 (over y_lo, x, core).
Axes of the slice: x: 4, y: 4 (y_hi: 2, y_lo: 2; y = y_hi * 2 + y_lo), z: 8, core: 2. Of those that a mesh axis runs over, the one named last changes fastest.
Arguments:
- final_hidden: bfloat16 [512, 4608], P('pipe', 'vocab'), may hold values from -6 to 6
- tied_table: bfloat16 [163840, 4608], P(('pipe', 'vocab')), may hold values from -1.2 to 1.2
- target_ids: int32 [512], replicated, may hold values from 0 to 163839
- input_ids: int32 [512], replicated, may hold values from 0 to 163839
- embed_cot: bfloat16 [512, 4608], P('pipe', 'vocab'), may hold values from -0.3125 to 0.3125
Outputs:
- grad_table: bfloat16 [163840, 4608], P(('pipe', 'vocab'))
- grad_hidden: float32 [512, 4608], P('pipe', 'vocab')
- token_loss: float32 [512], P('pipe')
All inputs are finite; a program needn't handle non-finite values.
Results may differ from a plain program's by a relative error of at most 0.01.
Values may be sent and summed in bfloat16 or wider, within the bound.
A program may use at most 128 MiB of HBM per device.

v0:
```python
import jax
import jax.numpy as jnp
from jax import lax
from jax.sharding import PartitionSpec as P

D = 4608


def local(final_hidden, tied_table, target_ids, input_ids, embed_cot):
    whole_h, whole_c = (
        lax.all_gather(final_hidden, "vocab", axis=1, tiled=True),
        lax.all_gather(embed_cot, "vocab", axis=1, tiled=True),
    )
    whole_h, whole_c = (
        lax.all_gather(whole_h, "pipe", axis=0, tiled=True),
        lax.all_gather(whole_c, "pipe", axis=0, tiled=True),
    )
    rows_dev = tied_table.shape[0]
    offset = lax.axis_index(("pipe", "vocab")) * rows_dev
    vocab_ids = offset + jnp.arange(rows_dev, dtype=jnp.int32)
    logits = jnp.einsum("td,vd->tv", whole_h, tied_table, preferred_element_type=jnp.float32)
    tanh_part = jnp.tanh(logits / 30.0)
    capped = 30.0 * tanh_part
    exponent = jnp.exp(capped)
    target_mask = vocab_ids[None, :] == target_ids[:, None]
    local_sum = jnp.sum(exponent, axis=1)
    local_target = jnp.sum(jnp.where(target_mask, capped, 0.0), axis=1)
    sum_exp, target_logit = lax.psum((local_sum, local_target), ("pipe", "vocab"))
    token_loss = jnp.log(sum_exp) - target_logit
    dlogits = (
        (exponent / sum_exp[:, None] - target_mask.astype(jnp.float32))
        * (1.0 - tanh_part * tanh_part)
    ).astype(jnp.bfloat16)
    head_grad = jnp.einsum("tv,td->vd", dlogits, whole_h, preferred_element_type=jnp.float32)
    input_mask = (vocab_ids[:, None] == input_ids[None, :]).astype(jnp.bfloat16)
    embed_grad = jnp.dot(input_mask, whole_c, preferred_element_type=jnp.float32)
    grad_table = (head_grad + float(D) ** 0.5 * embed_grad).astype(jnp.bfloat16)
    products = jnp.dot(dlogits, tied_table, preferred_element_type=jnp.float32)
    partial_value = lax.psum_scatter(
        products.astype(jnp.bfloat16), "vocab", scatter_dimension=1, tiled=True
    ).astype(jnp.float32)
    grad_hidden = lax.psum_scatter(partial_value, "pipe", scatter_dimension=0, tiled=True)
    held = final_hidden.shape[0]
    loss_shard = lax.dynamic_slice_in_dim(token_loss, lax.axis_index("pipe") * held, held)
    return (grad_table, grad_hidden, loss_shard)


def solution(mesh):
    placed = (P("pipe", "vocab"), P(("pipe", "vocab"), None), P(), P(), P("pipe", "vocab"))
    return jax.shard_map(
        local,
        mesh=mesh,
        in_specs=placed,
        out_specs=(P(("pipe", "vocab"), None), P("pipe", "vocab"), P("pipe")),
        check_vma=False,
    )
```

profile of v0, /device:TPU:2, one launch (start us, length us, event | category | flops | bytes accessed | tf_op | source)
XLA Modules:
  0.0 609.2 jit_solution(8618035419654364876)
XLA Ops:
  7.2 0.0 copy-start
  7.2 0.0 all-gather.5.cloned.1.call-start
  7.2 19.4 %all-gather = bf16[16,288,32]{1,2,0:T(8,128)(2,1)S(1)} all-gather(bf16[1,288,32]{1,2,0:T(8,128)(2,1)} %bitcast.20), channel_id=1, replica_groups=mesh['pipe'=16,'vocab'=16] {'vocab'}, dimensions={0}, use_global_device_ids=true | all-gather | bytes 313344 | tf_op jit(solution)/shard_map/all_gather | solution.py:11
  26.7 0.1 copy.12
  26.8 1.1 reshape.18
  27.9 0.0 all-gather.5.cloned.1.call-update
  27.9 0.0 reduce-scatter.5.cloned.1.call-start
  28.0 105.3 %all-gather.5.cloned.1.call-done = bf16[512,4608]{1,0:T(8,128)(2,1)} async-done(((bf16[32,4608]{1,0:T(8,128)(2,1)}), bf16[512,4608]{1,0:T(8,128)(2,1)}) %all-gather.5.cloned.1.call-update) | async-done | bytes 4718608 | tf_op jit(solution)/shard_map/all_gather | solution.py:15
  133.3 0.0 copy-done
  133.3 7.8 %fusion.4 = (f32[512]{0:T(512)S(1)}, f32[512]{0:T(512)S(1)}, f32[512,640]{1,0:T(8,128)S(1)}) fusion(s32[640]{0:T(1024)S(1)} %iota_add_fusion, s32[512]{0:T(512)S(1)} %copy-done, bf16[512,4608]{1,0:T(8,128)(2,1)} %all-gather.5.cloned.1.call-done, bf16[640,4608]{1,0:T(8,128)(2,1)} %param.6), kind=kOutput, calls=%fused_computation.9 | convolution fusion | flops 3021863936 | bytes 11936256 | tf_op jit(solution)/shard_map/td,vd->tv/dot_general | solution.py:21
  141.0 72.8 %all-reduce = (f32[512]{0:T(512)S(1)}, f32[512]{0:T(512)S(1)}) all-reduce(f32[512]{0:T(512)S(1)} %get-tuple-element.13, f32[512]{0:T(512)S(1)} %get-tuple-element.12), channel_id=1, replica_groups=mesh['pipe'=16,'vocab'=16] {'pipe','vocab'}, use_global_device_ids=true, to_apply=%region_1.2 | all-reduce | flops 1024 | bytes 8192 | tf_op jit(solution)/shard_map/psum | solution.py:28
  213.8 9.8 %convolution_convert_fusion = bf16[512,4608]{0,1:T(8,128)(2,1)} fusion(bf16[640,4608]{1,0:T(8,128)(2,1)} %param.6, f32[512,640]{1,0:T(8,128)S(1)} %get-tuple-element.16, s32[640]{0:T(1024)S(1)} %iota_add_fusion, f32[512]{0:T(512)S(1)} %get-tuple-element.14, s32[512]{0:T(512)S(1)} %copy-done), kind=kOutput, calls=%fused_computation.1 | convolution fusion | flops 3025207296 | bytes 11934208 | tf_op jit(solution)/shard_map/dot_general | solution.py:38
  223.6 0.0 copy-start.1
  223.6 0.0 reduce-scatter.5.cloned.1.call-update
  223.6 0.0 all-gather.7.cloned.1.call-start
  223.7 0.7 copy-done.1
  224.4 19.9 %all-gather.1 = bf16[16,288,32]{1,2,0:T(8,128)(2,1)S(1)} all-gather(bf16[1,288,32]{1,2,0:T(8,128)(2,1)S(1)} %bitcast.21), channel_id=1, replica_groups=mesh['pipe'=16,'vocab'=16] {'vocab'}, dimensions={0}, use_global_device_ids=true | all-gather | bytes 313344 | tf_op jit(solution)/shard_map/all_gather | solution.py:12
  244.3 0.1 copy.13
  244.4 1.1 reshape.20
  245.5 0.0 all-gather.7.cloned.1.call-update
  245.6 0.2 reduce-scatter.7.cloned.1.call-start
  245.8 10.2 %fusion.9 = f32[640,4608]{1,0:T(8,128)} fusion(bf16[512,4608]{1,0:T(8,128)(2,1)} %all-gather.5.cloned.1.call-done, f32[512,640]{1,0:T(8,128)S(1)} %get-tuple-element.16, s32[640]{0:T(1024)S(1)} %iota_add_fusion, f32[512]{0:T(512)S(1)} %get-tuple-element.14, s32[512]{0:T(512)S(1)} %copy-done), kind=kOutput, calls=%fused_computation.16 | convolution fusion | flops 3022848000 | bytes 17832448 | tf_op jit(solution)/shard_map/tv,td->vd/dot_general | solution.py:34
  256.0 0.0 copy-start.2
  256.0 32.3 %reduce-scatter.5.cloned.1.call-done = bf16[512,288]{0,1:T(8,128)(2,1)} async-done(((bf16[512,4608]{0,1:T(8,128)(2,1)}), bf16[512,288]{0,1:T(8,128)(2,1)}) %reduce-scatter.5.cloned.1.call-update) | async-done | bytes 294928 | tf_op jit(solution)/shard_map/reduce_scatter | solution.py:39
  288.3 2.0 copy.15
  290.3 0.0 reduce-scatter.7.cloned.1.call-update
  290.3 0.6 dynamic_slice.3
  290.9 106.2 %all-gather.7.cloned.1.call-done = bf16[512,4608]{1,0:T(8,128)(2,1)} async-done(((bf16[32,4608]{1,0:T(8,128)(2,1)}), bf16[512,4608]{1,0:T(8,128)(2,1)}) %all-gather.7.cloned.1.call-update) | async-done | bytes 4718608 | tf_op jit(solution)/shard_map/all_gather | solution.py:16
  397.1 0.0 copy-done.2
  397.1 9.3 %add_convert_fusion = bf16[640,4608]{1,0:T(8,128)(2,1)} fusion(f32[640,4608]{1,0:T(8,128)} %fusion.9, bf16[512,4608]{1,0:T(8,128)(2,1)} %all-gather.7.cloned.1.call-done, s32[512]{0:T(512)S(1)} %copy-done.2, s32[640]{0:T(1024)S(1)} %iota_add_fusion), kind=kOutput, calls=%fused_computation | convolution fusion | flops 3029073920 | bytes 22417920 | tf_op jit(solution)/shard_map/dot_general | solution.py:36
  406.3 196.3 %reduce-scatter.7.cloned.1.call-done = f32[32,288]{1,0:T(8,128)} async-done(((f32[512,288]{1,0:T(8,128)}), f32[32,288]{1,0:T(8,128)}) %reduce-scatter.7.cloned.1.call-update) | async-done | bytes 36880
  (2 shorter events, 0.0 us)
Async XLA Ops:
  7.2 126.1 %copy-start = (s32[512]{0:T(512)S(1)}, s32[512]{0:T(512)}, u32[]{:S(2)}) copy-start(s32[512]{0:T(512)} %param.7) | copy-start | bytes 6148
  7.2 126.1 %all-gather.5.cloned.1.call-start = ((), (), s32[]{:S(2)}) async-start(), calls=%async_computation.2 | async-start | bytes 5013504 | tf_op jit(solution)/shard_map/all_gather | solution.py:15
  27.9 260.3 %reduce-scatter.5.cloned.1.call-start = ((), (), s32[]{:S(2)}) async-start(), calls=%async_computation.4 | async-start | bytes 5013504 | tf_op jit(solution)/shard_map/reduce_scatter | solution.py:39
  223.6 0.7 copy-start.1
  223.6 173.4 %all-gather.7.cloned.1.call-start = ((), (), s32[]{:S(2)}) async-start(), calls=%async_computation.3 | async-start | bytes 5013504 | tf_op jit(solution)/shard_map/all_gather | solution.py:16
  245.6 357.1 %reduce-scatter.7.cloned.1.call-start = ((), (), s32[]{:S(2)}) async-start(), calls=%async_computation.5 | async-start | bytes 835584
  256.0 141.1 %copy-start.2 = (s32[512]{0:T(512)S(1)}, s32[512]{0:T(512)}, u32[]{:S(2)}) copy-start(s32[512]{0:T(512)} %param.8) | copy-start | bytes 6148
Sparse Core Ops, SparseCore 0:
  28.0 105.1 all-gather.4
  223.8 64.4 reduce-scatter.4
  290.9 106.1 all-gather.6
  401.3 201.2 reduce-scatter.6
where the time goes:
time: 610 us; the launch traced here: 609 us
  waiting for transfers between devices  440 us (72%)
  blocking collectives  112 us (18%)
  matrix products  37 us (6%)
  between operations  13.8 us (2%)
    unnamed x5, waiting for transfers between devices  196 us
    all_gather x1, waiting for transfers between devices, local(): lax.all_gather(whole_c, 'pipe', axis=0, tiled=True)  106 us
    all_gather x1, waiting for transfers between devices, local(): lax.all_gather(whole_h, 'pipe', axis=0, tiled=True)  105 us
    psum x1, blocking collectives, local(): lax.psum((local_sum, local_target), ('pipe', 'vocab'))  72.8 us
    reduce_scatter x1, waiting for transfers between devices, local(): lax.psum_scatter(products.astype(jnp.bfloat16), 'vocab', scatter_dimensio...  32.3 us
    all_gather x1, blocking collectives, local(): lax.all_gather(embed_cot, 'vocab', axis=1, tiled=True)  19.9 us
    all_gather x1, blocking collectives, local(): lax.all_gather(final_hidden, 'vocab', axis=1, tiled=True)  19.4 us
  transfers between devices with their start and end apart: 4, of which 4 were waited for; matrix products, arithmetic and copies ran while one was open for 4% of the time, Pallas kernels for 0%

commit v1 on v0

--- a/solution.py
+++ b/solution.py
@@ -12,7 +12,9 @@
         lax.all_gather(embed_cot, "vocab", axis=1, tiled=True),
     )
     whole_h, whole_c = (
-        lax.all_gather(whole_h, "pipe", axis=0, tiled=True),
+        jnp.concatenate(
+            lax.all_to_all(jnp.stack([whole_h] * lax.axis_size("pipe")), "pipe", 0, 0), axis=0
+        ),
         lax.all_gather(whole_c, "pipe", axis=0, tiled=True),
     )
     rows_dev = tied_table.shape[0]

time: 610 us -> 579 us (0.949)
  waiting for transfers between devices: 440 us -> 394 us
  starting transfers between devices: 0.35 us -> 10.1 us
    all_to_all x0 -> x1, waiting for transfers between devices: none -> 108 us  [local(): lax.all_to_all(jnp.stack([whole_h] * lax.axis_size('pipe')), 'pipe', 0, 0)]
    all_gather x1 -> x0, waiting for transfers between devices: 105 us -> none  [local(): lax.all_gather(whole_h, 'pipe', axis=0, tiled=True)]
    all_gather x1, waiting for transfers between devices: 106 us -> 55.3 us  [local(): lax.all_gather(whole_c, 'pipe', axis=0, tiled=True)]
    all_to_all x0 -> x1, starting transfers between devices: none -> 9.84 us  [local(): lax.all_to_all(jnp.stack([whole_h] * lax.axis_size('pipe')), 'pipe', 0, 0)]
    unnamed x5 -> x4, waiting for transfers between devices: 196 us -> 196 us
where the time goes in v1:
time: 579 us
  waiting for transfers between devices  394 us (68%)
  blocking collectives  114 us (20%)
  matrix products  37 us (6%)
  between operations  15.5 us (3%)
  starting transfers between devices  10.1 us (2%)
  local copies, waits for them, and re-layouts  7.66 us (1%)
    unnamed x4, waiting for transfers between devices  196 us
    all_to_all x1, waiting for transfers between devices, local(): lax.all_to_all(jnp.stack([whole_h] * lax.axis_size('pipe')), 'pipe', 0, 0)  108 us
    psum x1, blocking collectives, local(): lax.psum((local_sum, local_target), ('pipe', 'vocab'))  75.8 us
    all_gather x1, waiting for transfers between devices, local(): lax.all_gather(whole_c, 'pipe', axis=0, tiled=True)  55.3 us
    reduce_scatter x1, waiting for transfers between devices, local(): lax.psum_scatter(products.astype(jnp.bfloat16), 'vocab', scatter_dimensio...  34 us
    all_gather x1, blocking collectives, local(): lax.all_gather(final_hidden, 'vocab', axis=1, tiled=True)  19.4 us
    all_gather x1, blocking collectives, local(): lax.all_gather(embed_cot, 'vocab', axis=1, tiled=True)  19 us
  transfers between devices with their start and end apart: 4, of which 4 were waited for; matrix products, arithmetic and copies ran while one was open for 4% of the time, Pallas kernels for 0%

profile of v1, /device:TPU:2, one launch (start us, length us, event | category | flops | bytes accessed | tf_op | source)
XLA Modules:
  0.0 578.6 jit_solution(522896226984759603)
XLA Ops:
  8.0 19.4 %all-gather = bf16[16,288,32]{1,2,0:T(8,128)(2,1)S(1)} all-gather(bf16[1,288,32]{1,2,0:T(8,128)(2,1)} %bitcast.21), channel_id=1, replica_groups=mesh['pipe'=16,'vocab'=16] {'vocab'}, dimensions={0}, use_global_device_ids=true | all-gather | bytes 313344 | tf_op jit(solution)/shard_map/all_gather | solution.py:11
  27.4 0.1 copy.13
  27.6 0.4 reshape.24
  28.0 2.6 stack.2
  30.6 0.0 copy-start
  30.6 9.8 %all-to-all-start = ((bf16[16,32,4608]{2,1,0:T(8,128)(2,1)}), bf16[16,32,4608]{2,1,0:T(8,128)(2,1)}, u32[]{:S(2)}, u32[]{:S(2)}) async-start(bf16[16,32,4608]{2,1,0:T(8,128)(2,1)} %stack.2), calls=%async_computation | async-start | bytes 9437184 | tf_op jit(solution)/shard_map/all_to_all | solution.py:16
  40.4 0.0 reduce-scatter.5.cloned.1.call-start
  40.5 108.4 %all-to-all-done = bf16[16,32,4608]{2,1,0:T(8,128)(2,1)} async-done(((bf16[16,32,4608]{2,1,0:T(8,128)(2,1)}), bf16[16,32,4608]{2,1,0:T(8,128)(2,1)}, u32[]{:S(2)}, u32[]{:S(2)}) %all-to-all-start) | async-done | bytes 4718624 | tf_op jit(solution)/shard_map/all_to_all | solution.py:16
  148.9 0.0 copy-done
  148.9 7.8 %fusion.4 = (f32[512]{0:T(512)S(1)}, f32[512]{0:T(512)S(1)}, f32[512,640]{1,0:T(8,128)S(1)}) fusion(s32[640]{0:T(1024)S(1)} %iota_add_fusion, s32[512]{0:T(512)S(1)} %copy-done, bf16[512,4608]{1,0:T(8,128)(2,1)} %bitcast.3, bf16[640,4608]{1,0:T(8,128)(2,1)} %param.6), kind=kOutput, calls=%fused_computation.9 | convolution fusion | flops 3021863936 | bytes 11936256 | tf_op jit(solution)/shard_map/td,vd->tv/dot_general | solution.py:23
  156.7 75.8 %all-reduce = (f32[512]{0:T(512)S(1)}, f32[512]{0:T(512)S(1)}) all-reduce(f32[512]{0:T(512)S(1)} %get-tuple-element.13, f32[512]{0:T(512)S(1)} %get-tuple-element.12), channel_id=1, replica_groups=mesh['pipe'=16,'vocab'=16] {'pipe','vocab'}, use_global_device_ids=true, to_apply=%region_1.2 | all-reduce | flops 1024 | bytes 8192 | tf_op jit(solution)/shard_map/psum | solution.py:30
  232.4 9.8 %convolution_convert_fusion = bf16[512,4608]{0,1:T(8,128)(2,1)} fusion(bf16[640,4608]{1,0:T(8,128)(2,1)} %param.6, f32[512,640]{1,0:T(8,128)S(1)} %get-tuple-element.16, s32[640]{0:T(1024)S(1)} %iota_add_fusion, f32[512]{0:T(512)S(1)} %get-tuple-element.14, s32[512]{0:T(512)S(1)} %copy-done), kind=kOutput, calls=%fused_computation.1 | convolution fusion | flops 3025207296 | bytes 11934208 | tf_op jit(solution)/shard_map/dot_general | solution.py:40
  242.2 0.0 copy-start.1
  242.2 0.0 reduce-scatter.5.cloned.1.call-update
  242.2 0.0 all-gather.4.cloned.1.call-start
  242.3 0.7 copy-done.1
  242.9 19.0 %all-gather.1 = bf16[16,288,32]{1,2,0:T(8,128)(2,1)S(1)} all-gather(bf16[1,288,32]{1,2,0:T(8,128)(2,1)S(1)} %bitcast.22), channel_id=1, replica_groups=mesh['pipe'=16,'vocab'=16] {'vocab'}, dimensions={0}, use_global_device_ids=true | all-gather | bytes 313344 | tf_op jit(solution)/shard_map/all_gather | solution.py:12
  261.9 0.1 copy.14
  262.1 1.1 reshape.26
  263.2 0.0 all-gather.4.cloned.1.call-update
  263.2 0.2 reduce-scatter.7.cloned.1.call-start
  263.4 10.2 %fusion.9 = f32[640,4608]{1,0:T(8,128)} fusion(bf16[512,4608]{1,0:T(8,128)(2,1)} %bitcast.3, f32[512,640]{1,0:T(8,128)S(1)} %get-tuple-element.16, s32[640]{0:T(1024)S(1)} %iota_add_fusion, f32[512]{0:T(512)S(1)} %get-tuple-element.14, s32[512]{0:T(512)S(1)} %copy-done), kind=kOutput, calls=%fused_computation.16 | convolution fusion | flops 3022848000 | bytes 17832448 | tf_op jit(solution)/shard_map/tv,td->vd/dot_general | solution.py:36
  273.7 0.0 copy-start.2
  273.7 34.0 %reduce-scatter.5.cloned.1.call-done = bf16[512,288]{0,1:T(8,128)(2,1)} async-done(((bf16[512,4608]{0,1:T(8,128)(2,1)}), bf16[512,288]{0,1:T(8,128)(2,1)}) %reduce-scatter.5.cloned.1.call-update) | async-done | bytes 294928 | tf_op jit(solution)/shard_map/reduce_scatter | solution.py:41
  307.6 2.0 copy.16
  309.7 0.0 reduce-scatter.7.cloned.1.call-update
  309.7 0.6 dynamic_slice.3
  310.3 55.3 %all-gather.4.cloned.1.call-done = bf16[512,4608]{1,0:T(8,128)(2,1)} async-done(((bf16[32,4608]{1,0:T(8,128)(2,1)}), bf16[512,4608]{1,0:T(8,128)(2,1)}) %all-gather.4.cloned.1.call-update) | async-done | bytes 4718608 | tf_op jit(solution)/shard_map/all_gather | solution.py:18
  365.6 0.0 copy-done.2
  365.6 9.3 %add_convert_fusion = bf16[640,4608]{1,0:T(8,128)(2,1)} fusion(f32[640,4608]{1,0:T(8,128)} %fusion.9, bf16[512,4608]{1,0:T(8,128)(2,1)} %all-gather.4.cloned.1.call-done, s32[512]{0:T(512)S(1)} %copy-done.2, s32[640]{0:T(1024)S(1)} %iota_add_fusion), kind=kOutput, calls=%fused_computation | convolution fusion | flops 3029073920 | bytes 22417920 | tf_op jit(solution)/shard_map/dot_general | solution.py:38
  374.9 196.3 %reduce-scatter.7.cloned.1.call-done = f32[32,288]{1,0:T(8,128)} async-done(((f32[512,288]{1,0:T(8,128)}), f32[32,288]{1,0:T(8,128)}) %reduce-scatter.7.cloned.1.call-update) | async-done | bytes 36880
  (2 shorter events, 0.0 us)
Async XLA Ops:
  30.6 118.3 %copy-start = (s32[512]{0:T(512)S(1)}, s32[512]{0:T(512)}, u32[]{:S(2)}) copy-start(s32[512]{0:T(512)} %param.7) | copy-start | bytes 6148
  30.6 118.3 %all-to-all-start = ((bf16[16,32,4608]{2,1,0:T(8,128)(2,1)}), bf16[16,32,4608]{2,1,0:T(8,128)(2,1)}, u32[]{:S(2)}, u32[]{:S(2)}) async-start(bf16[16,32,4608]{2,1,0:T(8,128)(2,1)} %stack.2), calls=%async_computation | async-start | bytes 9437184 | tf_op jit(solution)/shard_map/all_to_all | solution.py:16
  40.4 267.2 %reduce-scatter.5.cloned.1.call-start = ((), (), s32[]{:S(2)}) async-start(), calls=%async_computation.4 | async-start | bytes 5013504 | tf_op jit(solution)/shard_map/reduce_scatter | solution.py:41
  242.2 0.7 copy-start.1
  242.2 123.4 %all-gather.4.cloned.1.call-start = ((), (), s32[]{:S(2)}) async-start(), calls=%async_computation.3 | async-start | bytes 5013504 | tf_op jit(solution)/shard_map/all_gather | solution.py:18
  263.2 308.0 %reduce-scatter.7.cloned.1.call-start = ((), (), s32[]{:S(2)}) async-start(), calls=%async_computation.5 | async-start | bytes 835584
  273.7 92.0 %copy-start.2 = (s32[512]{0:T(512)S(1)}, s32[512]{0:T(512)}, u32[]{:S(2)}) copy-start(s32[512]{0:T(512)} %param.8) | copy-start | bytes 6148
Sparse Core Ops, SparseCore 0:
  242.4 65.2 reduce-scatter.4
Sparse Core Ops, SparseCore 1:
  263.3 102.3 all-gather.3
  369.9 201.2 reduce-scatter.6
